TPU v7x, 32 devices: a whole 2x2x4 slice. The times are simulated.
32 devices in a mesh: row: 8 (over y, x, core), col: 4 (over z).
Axes of the slice: x: 2, y: 2, z: 4, core: 2. Of those that a mesh axis runs over, the one named last changes fastest.
Arguments:
- inverse: float32 [4096, 4096], P('row', 'col'), may hold values from -0.05 to 0.05
- owner: int32 [32], replicated, may hold values from 0 to 31, each once
- struct_parent: int32 [32], replicated, may hold values 0 or 1
- struct_child: int32 [32], replicated, may hold values 0 or 1
- panel_parent: float32 [4096, 1024], P('row', 'col'), may hold values from -1.5 to 1.5
- panel_child: float32 [4096, 1024], P('row', 'col'), may hold values from -1.5 to 1.5
- child_on_parent: float32 [1024, 1024], P('col'), may hold values from -0.1875 to 0.1875
- dinv_parent: float32 [1024, 1024], P('col'), may hold values from -6 to 6
- dinv_child: float32 [1024, 1024], P('col'), may hold values from -6 to 6
Outputs:
- row_parent: float32 [1024, 4096], P('col', 'row')
- inv_parent: float32 [1024, 1024], P('col')
- row_child: float32 [1024, 4096], P('col', 'row')
- inv_cross: float32 [1024, 1024], P('col')
- inv_child: float32 [1024, 1024], P('col')
Inputs may be any that keep to these rules, and one draw needn't show every extreme that they name: `owner`: each slot holds a different block.
All inputs are finite; a program needn't handle non-finite values.
Results may differ from a plain program's by a relative error of at most 0.000071.
Values sent between devices are 32-bit elements; how exact they have to be, the bound alone decides.
A program may use at most 128 MiB of HBM per device.

v0:
```python
import jax
import jax.numpy as jnp
from jax import lax
from jax.sharding import PartitionSpec as P

BLOCK_ROWS = 128
HIGHEST = lax.Precision.HIGHEST


def broadcast(block, axis, source):
    block = jnp.where(lax.axis_index(axis) == source, block, jnp.zeros_like(block))
    return lax.psum(block, axis)


def contract_first(left, right):
    return lax.dot_general(
        left, right, (((0,), (0,)), ((), ())), precision=HIGHEST, preferred_element_type=jnp.float32
    )


def contract_cross(left, right):
    return lax.dot_general(
        left, right, (((0,), (1,)), ((), ())), precision=HIGHEST, preferred_element_type=jnp.float32
    )


def matmul(left, right):
    return jnp.dot(left, right, precision=HIGHEST, preferred_element_type=jnp.float32)


def per_device(
    inverse,
    owner,
    struct_parent,
    struct_child,
    panel_parent,
    panel_child,
    child_on_parent,
    dinv_parent,
    dinv_child,
):
    rows_dev = inverse.shape[0]
    nblocks = owner.shape[0]
    ratio = lax.axis_size("row") // lax.axis_size("col")
    row_at = lax.axis_index("row")
    col_at = lax.axis_index("col")
    row_tiles = rows_dev // BLOCK_ROWS
    matches = owner[:, None] == jnp.arange(nblocks, dtype=jnp.int32)[None, :]
    live_parent = jnp.sum(jnp.where(matches, struct_parent[None, :], 0), axis=1)
    live_child = live_parent * jnp.sum(jnp.where(matches, struct_child[None, :], 0), axis=1)
    parent_rowblk = lax.dynamic_slice_in_dim(live_parent, row_at * row_tiles, row_tiles)
    child_rowblk = lax.dynamic_slice_in_dim(live_child, row_at * row_tiles, row_tiles)
    mask_parent = jnp.repeat(parent_rowblk.astype(jnp.float32), BLOCK_ROWS)
    mask_child = jnp.repeat(child_rowblk.astype(jnp.float32), BLOCK_ROWS)
    masked_parent = panel_parent * mask_parent[:, None]
    masked_child = panel_child * mask_child[:, None]
    full_parent, full_child = (
        lax.all_gather(masked_parent, "col", axis=1, tiled=True),
        lax.all_gather(masked_child, "col", axis=1, tiled=True),
    )
    parent_pieces = []
    child_pieces = []
    for offset in range(ratio):
        got_parent, got_child = (
            broadcast(full_parent, "row", ratio * col_at + offset),
            broadcast(full_child, "row", ratio * col_at + offset),
        )
        parent_pieces.append(got_parent)
        child_pieces.append(got_child)
    column_parent = jnp.concatenate(parent_pieces, axis=0)
    column_child = jnp.concatenate(child_pieces, axis=0)

    def region_term(panel):
        return contract_cross(panel, inverse)

    row_parent = (
        -lax.psum_scatter(region_term(column_parent), "col", scatter_dimension=0, tiled=True)
        * mask_parent[None, :]
    )
    sum_parent, sum_cross = lax.psum(
        (matmul(row_parent, full_parent), matmul(row_parent, full_child)), "row"
    )
    inv_parent = dinv_parent - sum_parent
    parent_full = lax.all_gather(child_on_parent, "col", axis=0, tiled=True)
    inv_cross = -(sum_cross + matmul(inv_parent, parent_full))
    row_child = (
        -lax.psum_scatter(
            region_term(column_child) + contract_first(child_on_parent, row_parent),
            "col",
            scatter_dimension=0,
            tiled=True,
        )
        * mask_child[None, :]
    )
    sum_child = lax.psum(matmul(row_child, full_child), "row")
    cross_term = lax.psum_scatter(
        contract_first(inv_cross, child_on_parent), "col", scatter_dimension=0, tiled=True
    )
    inv_child = dinv_child - sum_child - cross_term
    return (row_parent, inv_parent, row_child, inv_cross, inv_child)


def solution(mesh):
    return jax.shard_map(
        per_device,
        mesh=mesh,
        in_specs=(
            P("row", "col"),
            P(),
            P(),
            P(),
            P("row", "col"),
            P("row", "col"),
            P("col", None),
            P("col", None),
            P("col", None),
        ),
        out_specs=(
            P("col", "row"),
            P("col", None),
            P("col", "row"),
            P("col", None),
            P("col", None),
        ),
        check_vma=False,
    )
```

profile of v0, /device:TPU:0, one launch (start us, length us, event | category | flops | bytes accessed | tf_op | source)
XLA Modules:
  0.0 599.8 jit_solution(15787337251794330934)
XLA Ops:
  7.2 1.0 select_reduce_fusion
  8.4 2.0 broadcast_multiply_fusion
  10.6 2.0 broadcast_multiply_fusion.1
  12.7 46.3 %all-gather.6.cloned.1.call-done = f32[512,1024]{1,0:T(8,128)} async-done(((f32[512,256]{1,0:T(8,128)}), f32[512,1024]{1,0:T(8,128)}) %all-gather.6.cloned.1.call-update) | async-done | bytes 2097168 | tf_op jit(solution)/shard_map/all_gather | solution.py:59
  58.9 4.2 broadcast_select_fusion.1
  63.2 42.4 %all-gather.4.cloned.1.call-done = f32[512,1024]{1,0:T(8,128)} async-done(((f32[512,256]{1,0:T(8,128)}), f32[512,1024]{1,0:T(8,128)}) %all-gather.4.cloned.1.call-update) | async-done | bytes 2097168 | tf_op jit(solution)/shard_map/all_gather | solution.py:58
  105.6 4.2 broadcast_select_fusion.3
  109.9 125.1 %all-reduce.7.cloned.1.call-done = (f32[512,1024]{1,0:T(8,128)}, f32[512,1024]{1,0:T(8,128)}, f32[512,1024]{1,0:T(8,128)}, f32[512,1024]{1,0:T(8,128)}) async-done(((f32[512,1024]{1,0:T(8,128)}, f32[512,1024]{1,0:T(8,128)}, f32[512,1024]{1,0:T(8,128)}, f32[512,1024]{1,0:T(8,128)}), (f32[512,1024]{1,0:T(8,128)}, f32[512,1024]{1,0:T(8,128)}, f32[512,1024]{1,0:T(8,128)}, ...) | async-done | bytes 8388624 | tf_op jit(solution)/shard_map/psum | solution.py:12
  235.0 16.0 %fusion = f32[1024,512]{1,0:T(8,128)} fusion(f32[512,1024]{1,0:T(8,128)S(1)} %copy-done, f32[512,1024]{1,0:T(8,128)} %get-tuple-element.10, f32[512,1024]{1,0:T(8,128)} %get-tuple-element.11), kind=kOutput, calls=%fused_computation | convolution fusion | flops 6443499520 | bytes 8388608 | tf_op jit(solution)/shard_map/dot_general | solution.py:22
  251.0 0.2 reduce-scatter.6.cloned.1.call-start
  251.2 16.1 %fusion.4 = f32[1024,512]{1,0:T(8,128)} fusion(f32[512,1024]{1,0:T(8,128)S(1)} %copy-done, f32[512,1024]{1,0:T(8,128)} %get-tuple-element.12, f32[512,1024]{1,0:T(8,128)} %get-tuple-element.13), kind=kOutput, calls=%fused_computation.4 | convolution fusion | flops 6443499520 | bytes 8388608 | tf_op jit(solution)/shard_map/dot_general | solution.py:22
  267.3 27.6 %reduce-scatter.4.cloned.1.call-done = f32[256,512]{1,0:T(8,128)} async-done(((f32[1024,512]{1,0:T(8,128)}), f32[256,512]{1,0:T(8,128)}) %reduce-scatter.4.cloned.1.call-update) | async-done | bytes 524304 | tf_op jit(solution)/shard_map/reduce_scatter | solution.py:77
  294.9 1.1 negate_multiply_fusion.1
  296.0 0.8 copy-done.4
  296.8 4.9 bitcast_add_fusion
  301.7 0.3 all-reduce.5.cloned.1.call-start
  302.0 0.7 copy-done.5
  302.7 4.6 fusion.12
  307.3 2.9 fusion.11
  310.2 34.5 %reduce-scatter.6.cloned.1.call-done = f32[256,512]{1,0:T(8,128)} async-done(((f32[1024,512]{1,0:T(8,128)}), f32[256,512]{1,0:T(8,128)}) %reduce-scatter.6.cloned.1.call-update) | async-done | bytes 524304 | tf_op jit(solution)/shard_map/reduce_scatter | solution.py:87
  344.7 1.1 negate_multiply_fusion
  345.8 0.8 copy-done.8
  346.6 4.5 fusion.13
  351.1 0.7 all-gather.8.cloned.1.call-update
  351.9 68.0 %all-reduce.5.cloned.1.call-done = (f32[256,1024]{1,0:T(8,128)}, f32[256,1024]{1,0:T(8,128)}, f32[256,1024]{1,0:T(8,128)}) async-done(((f32[256,1024]{1,0:T(8,128)}, f32[256,1024]{1,0:T(8,128)}, f32[256,1024]{1,0:T(8,128)}), (f32[256,1024]{1,0:T(8,128)}, f32[256,1024]{1,0:T(8,128)}, f32[256,1024]{1,0:T(8,128)})) %all-reduce.5.cloned.1.call-update) | async-done | bytes 3145744 | tf_op jit(solution)/shard_map/psum | solution.py:80
  419.9 1.7 sub.9
  421.5 80.7 %all-gather.8.cloned.1.call-done = f32[1024,1024]{1,0:T(8,128)} async-done(((f32[256,1024]{1,0:T(8,128)}), f32[1024,1024]{1,0:T(8,128)}) %all-gather.8.cloned.1.call-update) | async-done | bytes 4194320 | tf_op jit(solution)/shard_map/all_gather | solution.py:84
  502.3 6.3 %fusion.8 = f32[256,1024]{1,0:T(8,128)S(1)} fusion(f32[256,1024]{1,0:T(8,128)} %get-tuple-element.8, f32[256,1024]{1,0:T(8,128)S(1)} %sub.9, f32[1024,1024]{1,0:T(8,128)} %all-gather.8.cloned.1.call-done), kind=kOutput, calls=%fused_computation.10 | convolution fusion | flops 3221749760 | bytes 7340032 | tf_op jit(solution)/shard_map/dot_general | solution.py:28
  508.6 1.0 copy-done.7
  509.6 5.1 fusion.14
  514.7 75.4 %reduce-scatter.8.cloned.1.call-done = f32[256,1024]{1,0:T(8,128)} async-done(((f32[1024,1024]{1,0:T(8,128)}), f32[256,1024]{1,0:T(8,128)}) %reduce-scatter.8.cloned.1.call-update) | async-done | bytes 1048592 | tf_op jit(solution)/shard_map/reduce_scatter | solution.py:96
  590.1 2.8 subtract_subtract_fusion
  (34 shorter events, 0.7 us)
Async XLA Ops:
  7.2 227.8 %copy-start = (f32[512,1024]{1,0:T(8,128)S(1)}, f32[512,1024]{1,0:T(8,128)}, u32[]{:S(2)}) copy-start(f32[512,1024]{1,0:T(8,128)} %param.9) | copy-start | bytes 6291460
  7.2 51.8 %all-gather.6.cloned.1.call-start = ((), (), s32[]{:S(2)}) async-start(), calls=%async_computation.5 | async-start | bytes 2621440 | tf_op jit(solution)/shard_map/all_gather | solution.py:59
  10.4 95.2 %all-gather.4.cloned.1.call-start = ((), (), s32[]{:S(2)}) async-start(), calls=%async_computation.3 | async-start | bytes 2621440 | tf_op jit(solution)/shard_map/all_gather | solution.py:58
  12.6 222.4 %all-reduce.7.cloned.1.call-start = ((), (), s32[]{:S(2)}) async-start(), calls=%async_computation.10 | async-start | bytes 16777216 | tf_op jit(solution)/shard_map/psum | solution.py:12
  109.8 185.1 %reduce-scatter.4.cloned.1.call-start = ((), (), s32[]{:S(2)}) async-start(), calls=%async_computation.4 | async-start | bytes 2621440 | tf_op jit(solution)/shard_map/reduce_scatter | solution.py:77
  251.0 93.7 %reduce-scatter.6.cloned.1.call-start = ((), (), s32[]{:S(2)}) async-start(), calls=%async_computation.6 | async-start | bytes 2621440 | tf_op jit(solution)/shard_map/reduce_scatter | solution.py:87
  251.2 45.6 %copy-start.1 = (f32[256,1024]{1,0:T(8,128)S(1)}, f32[256,1024]{1,0:T(8,128)}, u32[]{:S(2)}) copy-start(f32[256,1024]{1,0:T(8,128)} %param.15) | copy-start | bytes 3145732
  296.0 0.8 copy-start.4
  301.7 1.0 copy-start.5
  301.7 118.1 %all-reduce.5.cloned.1.call-start = ((), (), s32[]{:S(2)}) async-start(), calls=%async_computation.9 | async-start | bytes 6291456 | tf_op jit(solution)/shard_map/psum | solution.py:80
  302.7 4.6 copy-start.3
  345.8 0.8 copy-start.8
  351.1 151.2 %all-gather.8.cloned.1.call-start = ((), (), s32[]{:S(2)}) async-start(), calls=%async_computation.7 | async-start | bytes 5242880 | tf_op jit(solution)/shard_map/all_gather | solution.py:84
  351.8 238.3 %reduce-scatter.8.cloned.1.call-start = ((), (), s32[]{:S(2)}) async-start(), calls=%async_computation.8 | async-start | bytes 5242880 | tf_op jit(solution)/shard_map/reduce_scatter | solution.py:96
  421.5 87.1 %copy-start.6 = (f32[256,1024]{1,0:T(8,128)}, f32[256,1024]{1,0:T(8,128)S(1)}, u32[]{:S(2)}) copy-start(f32[256,1024]{1,0:T(8,128)S(1)} %sub.9) | copy-start | bytes 3145732
  502.3 7.3 %copy-start.2 = (f32[256,1024]{1,0:T(8,128)S(1)}, f32[256,1024]{1,0:T(8,128)}, u32[]{:S(2)}) copy-start(f32[256,1024]{1,0:T(8,128)} %param.15) | copy-start | bytes 3145732
  508.6 1.0 copy-start.7
  514.7 75.5 %copy-start.9 = (f32[256,1024]{1,0:T(8,128)S(1)}, f32[256,1024]{1,0:T(8,128)}, u32[]{:S(2)}) copy-start(f32[256,1024]{1,0:T(8,128)} %param.17) | copy-start | bytes 3145732
Sparse Core Ops, SparseCore 0:
  10.5 48.3 all-gather.5
  61.1 44.4 all-gather.3
  109.9 125.0 all-reduce.6
  251.1 43.7 reduce-scatter.3
  301.8 42.8 reduce-scatter.5
  351.2 68.6 all-reduce.4
  421.4 80.8 all-gather.7
  514.8 75.2 reduce-scatter.7
where the time goes:
time: 600 us
  waiting for transfers between devices  501 us (84%)
  matrix products  60.2 us (10%)
  other arithmetic  20.2 us (3%)
  between operations  14.3 us (2%)
    psum x1, waiting for transfers between devices, broadcast(): return lax.psum(block, axis)  125 us
    all_gather x1, waiting for transfers between devices, per_device(): parent_full = lax.all_gather(child_on_parent, 'col', axis=0, tiled=True)  80.7 us
    reduce_scatter x1, waiting for transfers between devices, per_device(): lax.psum_scatter(contract_first(inv_cross, child_on_parent), 'col', scatt...  75.4 us
    psum x1, waiting for transfers between devices, per_device(): lax.psum((matmul(row_parent, full_parent), matmul(row_parent, full_child)...  68 us
    all_gather x1, waiting for transfers between devices, per_device(): lax.all_gather(masked_child, 'col', axis=1, tiled=True)  46.3 us
    all_gather x1, waiting for transfers between devices, per_device(): lax.all_gather(masked_parent, 'col', axis=1, tiled=True)  42.4 us
    reduce_scatter x1, waiting for transfers between devices, per_device(): lax.psum_scatter(region_term(column_child) + contract_first(child_on_pare...  34.5 us
    dot_general x2, matrix products, contract_cross(): lax.dot_general(left, right, (((0,), (1,)), ((), ())), precision=HIGHEST,...  32 us
  transfers between devices with their start and end apart: 8, of which 8 were waited for; matrix products, arithmetic and copies ran while one was open for 5% of the time, Pallas kernels for 0%

commit v1 on v0

--- a/solution.py
+++ b/solution.py
@@ -9,7 +9,7 @@
 
 def broadcast(block, axis, source):
     block = jnp.where(lax.axis_index(axis) == source, block, jnp.zeros_like(block))
-    return lax.psum(block, axis)
+    return jnp.sum(lax.all_gather(block, axis), axis=0)
 
 
 def contract_first(left, right):

time: 600 us -> 831 us (1.39); the launches traced: 600 us -> 821 us
  waiting for transfers between devices: 501 us -> 675 us
  other arithmetic: 20.2 us -> 57.6 us
  starting transfers between devices: 0.73 us -> 9.99 us
    all_gather x0 -> x4, waiting for transfers between devices: none -> 306 us  [broadcast(): return jnp.sum(lax.all_gather(block, axis), axis=0)]
    psum x1 -> x0, waiting for transfers between devices: 125 us -> none  [broadcast(): return lax.psum(block, axis)]
    reduce_sum x0 -> x4, other arithmetic: none -> 37.3 us  [broadcast(): return jnp.sum(lax.all_gather(block, axis), axis=0)]
    reduce_scatter x1, starting transfers between devices: 0.22 us -> 9.4 us  [per_device(): lax.psum_scatter(region_term(column_child) + contract_first(child_on_pare...]
  transfers between devices with their start and end apart: 8 -> 11, of which waited for: 8 -> 11; matrix products, arithmetic and copies ran while one was open for 5% -> 11% of each run, Pallas kernels for 0% -> 0%
where the time goes in v1:
time: 831 us; the launch traced here: 821 us
  waiting for transfers between devices  675 us (81%)
  matrix products  60.4 us (7%)
  other arithmetic  57.6 us (7%)
  between operations  14.4 us (2%)
  starting transfers between devices  9.99 us (1%)
    all_gather x4, waiting for transfers between devices, broadcast(): return jnp.sum(lax.all_gather(block, axis), axis=0)  306 us
    all_gather x1, waiting for transfers between devices, per_device(): parent_full = lax.all_gather(child_on_parent, 'col', axis=0, tiled=True)  80.6 us
    reduce_scatter x1, waiting for transfers between devices, per_device(): lax.psum_scatter(contract_first(inv_cross, child_on_parent), 'col', scatt...  75.4 us
    psum x1, waiting for transfers between devices, per_device(): lax.psum((matmul(row_parent, full_parent), matmul(row_parent, full_child)...  68.2 us
    all_gather x1, waiting for transfers between devices, per_device(): lax.all_gather(masked_parent, 'col', axis=1, tiled=True)  46.3 us
    all_gather x1, waiting for transfers between devices, per_device(): lax.all_gather(masked_child, 'col', axis=1, tiled=True)  41.7 us
    reduce_sum x4, other arithmetic, broadcast(): return jnp.sum(lax.all_gather(block, axis), axis=0)  37.3 us
    reduce_scatter x1, waiting for transfers between devices, per_device(): lax.psum_scatter(region_term(column_child) + contract_first(child_on_pare...  34.5 us
  transfers between devices with their start and end apart: 11, of which 11 were waited for; matrix products, arithmetic and copies ran while one was open for 11% of the time, Pallas kernels for 0%

profile of v1, /device:TPU:0, one launch (start us, length us, event | category | flops | bytes accessed | tf_op | source)
XLA Modules:
  0.0 821.2 jit_solution(7396953306050971827)
XLA Ops:
  8.4 2.0 broadcast_multiply_fusion.1
  10.6 2.0 broadcast_multiply_fusion
  12.7 46.3 %all-gather.12.cloned.1.call-done = f32[512,1024]{1,0:T(8,128)} async-done(((f32[512,256]{1,0:T(8,128)}), f32[512,1024]{1,0:T(8,128)}) %all-gather.12.cloned.1.call-update) | async-done | bytes 2097168 | tf_op jit(solution)/shard_map/all_gather | solution.py:58
  58.9 4.3 broadcast_select_fusion.3
  63.9 41.7 %all-gather.14.cloned.1.call-done = f32[512,1024]{1,0:T(8,128)} async-done(((f32[512,256]{1,0:T(8,128)}), f32[512,1024]{1,0:T(8,128)}) %all-gather.14.cloned.1.call-update) | async-done | bytes 2097168 | tf_op jit(solution)/shard_map/all_gather | solution.py:59
  105.6 4.3 broadcast_select_fusion.1
  110.5 85.5 %all-gather.18.cloned.1.call-done = f32[4096,1024]{1,0:T(8,128)} async-done(((f32[512,1024]{1,0:T(8,128)}), f32[4096,1024]{1,0:T(8,128)}) %all-gather.18.cloned.1.call-update) | async-done | bytes 16777232 | tf_op jit(solution)/shard_map/all_gather | solution.py:12
  196.0 9.3 %reduce_sum.55 = f32[512,1024]{1,0:T(8,128)} reduce(f32[8,512,1024]{2,1,0:T(8,128)} %bitcast.24, f32[]{:T(128)} %constant.20.clone.1), dimensions={0}, to_apply=%region_1.2 | reduce | flops 3670016 | bytes 18874372 | tf_op jit(solution)/shard_map/reduce_sum | solution.py:12
  205.3 82.2 %all-gather.20.cloned.1.call-done = f32[4096,1024]{1,0:T(8,128)} async-done(((f32[512,1024]{1,0:T(8,128)}), f32[4096,1024]{1,0:T(8,128)}) %all-gather.20.cloned.1.call-update) | async-done | bytes 16777232 | tf_op jit(solution)/shard_map/all_gather | solution.py:12
  287.5 9.3 %reduce_sum.56 = f32[512,1024]{1,0:T(8,128)} reduce(f32[8,512,1024]{2,1,0:T(8,128)} %bitcast.25, f32[]{:T(128)} %constant.20.clone.1), dimensions={0}, to_apply=%region_2.3 | reduce | flops 3670016 | bytes 18874372 | tf_op jit(solution)/shard_map/reduce_sum | solution.py:12
  296.8 16.3 %fusion = f32[1024,512]{1,0:T(8,128)} fusion(f32[512,1024]{1,0:T(8,128)S(1)} %copy-done, f32[512,1024]{1,0:T(8,128)} %reduce_sum.56, f32[512,1024]{1,0:T(8,128)} %reduce_sum.55), kind=kOutput, calls=%fused_computation | convolution fusion | flops 6443499520 | bytes 8388608 | tf_op jit(solution)/shard_map/dot_general | solution.py:22
  313.2 9.4 %reduce-scatter.6.cloned.1.call-start = ((), (), s32[]{:S(2)}) async-start(), calls=%async_computation.6 | async-start | bytes 2621440 | tf_op jit(solution)/shard_map/reduce_scatter | solution.py:87
  322.6 56.4 %all-gather.22.cloned.1.call-done = f32[4096,1024]{1,0:T(8,128)} async-done(((f32[512,1024]{1,0:T(8,128)}), f32[4096,1024]{1,0:T(8,128)}) %all-gather.22.cloned.1.call-update) | async-done | bytes 16777232 | tf_op jit(solution)/shard_map/all_gather | solution.py:12
  379.0 9.4 %reduce_sum.58 = f32[512,1024]{1,0:T(8,128)} reduce(f32[8,512,1024]{2,1,0:T(8,128)} %bitcast.26, f32[]{:T(128)} %constant.20.clone.1), dimensions={0}, to_apply=%region_6.7 | reduce | flops 3670016 | bytes 18874372 | tf_op jit(solution)/shard_map/reduce_sum | solution.py:12
  388.4 82.1 %all-gather.24.cloned.1.call-done = f32[4096,1024]{1,0:T(8,128)} async-done(((f32[512,1024]{1,0:T(8,128)}), f32[4096,1024]{1,0:T(8,128)}) %all-gather.24.cloned.1.call-update) | async-done | bytes 16777232 | tf_op jit(solution)/shard_map/all_gather | solution.py:12
  470.5 9.3 %reduce_sum.59 = f32[512,1024]{1,0:T(8,128)} reduce(f32[8,512,1024]{2,1,0:T(8,128)} %bitcast.27, f32[]{:T(128)} %constant.20.clone.1), dimensions={0}, to_apply=%region_7.8 | reduce | flops 3670016 | bytes 18874372 | tf_op jit(solution)/shard_map/reduce_sum | solution.py:12
  479.8 16.0 %fusion.4 = f32[1024,512]{1,0:T(8,128)} fusion(f32[512,1024]{1,0:T(8,128)S(1)} %copy-done, f32[512,1024]{1,0:T(8,128)} %reduce_sum.59, f32[512,1024]{1,0:T(8,128)} %reduce_sum.58), kind=kOutput, calls=%fused_computation.4 | convolution fusion | flops 6443499520 | bytes 8388608 | tf_op jit(solution)/shard_map/dot_general | solution.py:22
  495.8 20.6 %reduce-scatter.4.cloned.1.call-done = f32[256,512]{1,0:T(8,128)} async-done(((f32[1024,512]{1,0:T(8,128)}), f32[256,512]{1,0:T(8,128)}) %reduce-scatter.4.cloned.1.call-update) | async-done | bytes 524304 | tf_op jit(solution)/shard_map/reduce_scatter | solution.py:77
  516.5 1.1 negate_multiply_fusion.1
  518.4 4.8 bitcast_add_fusion
  524.2 4.6 fusion.12
  528.8 2.9 fusion.11
  531.7 34.5 %reduce-scatter.6.cloned.1.call-done = f32[256,512]{1,0:T(8,128)} async-done(((f32[1024,512]{1,0:T(8,128)}), f32[256,512]{1,0:T(8,128)}) %reduce-scatter.6.cloned.1.call-update) | async-done | bytes 524304 | tf_op jit(solution)/shard_map/reduce_scatter | solution.py:87
  566.2 1.1 negate_multiply_fusion
  568.1 4.5 fusion.13
  573.2 68.2 %all-reduce.3.cloned.1.call-done = (f32[256,1024]{1,0:T(8,128)}, f32[256,1024]{1,0:T(8,128)}, f32[256,1024]{1,0:T(8,128)}) async-done(((f32[256,1024]{1,0:T(8,128)}, f32[256,1024]{1,0:T(8,128)}, f32[256,1024]{1,0:T(8,128)}), (f32[256,1024]{1,0:T(8,128)}, f32[256,1024]{1,0:T(8,128)}, f32[256,1024]{1,0:T(8,128)})) %all-reduce.3.cloned.1.call-update) | async-done | bytes 3145744 | tf_op jit(solution)/shard_map/psum | solution.py:80
  641.4 1.7 sub.9
  643.1 80.6 %all-gather.16.cloned.1.call-done = f32[1024,1024]{1,0:T(8,128)} async-done(((f32[256,1024]{1,0:T(8,128)}), f32[1024,1024]{1,0:T(8,128)}) %all-gather.16.cloned.1.call-update) | async-done | bytes 4194320 | tf_op jit(solution)/shard_map/all_gather | solution.py:84
  723.6 6.3 fusion.8
  731.0 5.1 fusion.14
  736.1 75.4 %reduce-scatter.8.cloned.1.call-done = f32[256,1024]{1,0:T(8,128)} async-done(((f32[1024,1024]{1,0:T(8,128)}), f32[256,1024]{1,0:T(8,128)}) %reduce-scatter.8.cloned.1.call-update) | async-done | bytes 1048592 | tf_op jit(solution)/shard_map/reduce_scatter | solution.py:96
  811.5 2.8 subtract_subtract_fusion
  (47 shorter events, 7.0 us)
Async XLA Ops:
  7.2 289.7 %copy-start = (f32[512,1024]{1,0:T(8,128)S(1)}, f32[512,1024]{1,0:T(8,128)}, u32[]{:S(2)}) copy-start(f32[512,1024]{1,0:T(8,128)} %param.9) | copy-start | bytes 6291460
  7.2 51.7 %all-gather.12.cloned.1.call-start = ((), (), s32[]{:S(2)}) async-start(), calls=%async_computation.3 | async-start | bytes 2621440 | tf_op jit(solution)/shard_map/all_gather | solution.py:58
  10.4 95.2 %all-gather.14.cloned.1.call-start = ((), (), s32[]{:S(2)}) async-start(), calls=%async_computation.5 | async-start | bytes 2621440 | tf_op jit(solution)/shard_map/all_gather | solution.py:59
  12.6 183.4 %all-gather.18.cloned.1.call-start = ((), (), s32[]{:S(2)}) async-start(), calls=%async_computation.9 | async-start | bytes 18874368 | tf_op jit(solution)/shard_map/all_gather | solution.py:12
  63.2 224.3 %all-gather.20.cloned.1.call-start = ((), (), s32[]{:S(2)}) async-start(), calls=%async_computation.10 | async-start | bytes 18874368 | tf_op jit(solution)/shard_map/all_gather | solution.py:12
  63.8 315.2 %all-gather.22.cloned.1.call-start = ((), (), s32[]{:S(2)}) async-start(), calls=%async_computation.11 | async-start | bytes 18874368 | tf_op jit(solution)/shard_map/all_gather | solution.py:12
  109.9 360.6 %all-gather.24.cloned.1.call-start = ((), (), s32[]{:S(2)}) async-start(), calls=%async_computation.12 | async-start | bytes 18874368 | tf_op jit(solution)/shard_map/all_gather | solution.py:12
  110.5 406.0 %reduce-scatter.4.cloned.1.call-start = ((), (), s32[]{:S(2)}) async-start(), calls=%async_computation.4 | async-start | bytes 2621440 | tf_op jit(solution)/shard_map/reduce_scatter | solution.py:77
  313.2 253.0 %reduce-scatter.6.cloned.1.call-start = ((), (), s32[]{:S(2)}) async-start(), calls=%async_computation.6 | async-start | bytes 2621440 | tf_op jit(solution)/shard_map/reduce_scatter | solution.py:87
  479.8 38.6 %copy-start.1 = (f32[256,1024]{1,0:T(8,128)S(1)}, f32[256,1024]{1,0:T(8,128)}, u32[]{:S(2)}) copy-start(f32[256,1024]{1,0:T(8,128)} %param.15) | copy-start | bytes 3145732
  517.6 0.8 copy-start.4
  523.2 1.0 copy-start.5
  523.2 118.2 %all-reduce.3.cloned.1.call-start = ((), (), s32[]{:S(2)}) async-start(), calls=%async_computation.13 | async-start | bytes 6291456 | tf_op jit(solution)/shard_map/psum | solution.py:80
  524.2 4.6 copy-start.3
  567.3 0.8 copy-start.8
  572.5 151.1 %all-gather.16.cloned.1.call-start = ((), (), s32[]{:S(2)}) async-start(), calls=%async_computation.7 | async-start | bytes 5242880 | tf_op jit(solution)/shard_map/all_gather | solution.py:84
  573.1 238.4 %reduce-scatter.8.cloned.1.call-start = ((), (), s32[]{:S(2)}) async-start(), calls=%async_computation.8 | async-start | bytes 5242880 | tf_op jit(solution)/shard_map/reduce_scatter | solution.py:96
  643.1 86.9 %copy-start.6 = (f32[256,1024]{1,0:T(8,128)}, f32[256,1024]{1,0:T(8,128)S(1)}, u32[]{:S(2)}) copy-start(f32[256,1024]{1,0:T(8,128)S(1)} %sub.9) | copy-start | bytes 3145732
  723.6 7.3 copy-start.2
  730.0 1.0 copy-start.7
  736.0 75.5 %copy-start.9 = (f32[256,1024]{1,0:T(8,128)S(1)}, f32[256,1024]{1,0:T(8,128)}, u32[]{:S(2)}) copy-start(f32[256,1024]{1,0:T(8,128)} %param.17) | copy-start | bytes 3145732
Sparse Core Ops, SparseCore 0:
  10.5 48.3 all-gather.11
  61.1 44.4 all-gather.13
  107.5 88.5 all-gather.17
  197.8 89.7 all-gather.19
  289.3 89.7 all-gather.21
  380.8 89.7 all-gather.23
  472.8 43.6 reduce-scatter.3
  523.3 42.8 reduce-scatter.5
  572.7 68.6 all-reduce.2
  642.8 80.8 all-gather.15
  736.2 75.2 reduce-scatter.7
